TPU v7x, 32 devices: a whole 2x2x4 slice. The times are simulated.
32 devices in a mesh: group: 4 (over z), member: 8 (over y, x, core).
Axes of the slice: x: 2, y: 2, z: 4, core: 2. Of those that a mesh axis runs over, the one named last changes fastest.
Arguments:
- source: bfloat16 [32768, 256], P(('group', 'member')), may hold values from -6 to 6
- target: bfloat16 [8192, 256], P(('group', 'member')), may hold values from -6 to 6
- pair_source: int32 [32, 32], P(('group', 'member')), may hold values from 0 to 3, as said below
- pair_target: int32 [32, 32], P(('group', 'member')), may hold values from 0 to 15, as said below
- pair_count: int32 [32], P(('group', 'member')), may hold values from 4 to 32, as said below
Outputs:
- log_source: float32 [32768], P(('group', 'member'))
- log_target: float32 [8192], P(('group', 'member'))
Inputs may be any that keep to these rules, and one draw needn't show every extreme that they name: `pair_source`: each entry is the device's own source tile, 0 to 3; slots 0 to 3 name each of them once, and no (source tile, window tile) pair stands twice on one device. `pair_target`: window index of the pair's target tile; on every device slot 0 names the device's own target tile (index equal to its member index). `pair_count`: at least 4; in every group one device has exactly 32.
All inputs are finite; a program needn't handle non-finite values.
Results may differ from a plain program's by a relative error of at most 0.0031.
Values may be sent and summed in bfloat16 or wider, within the bound.
No kernel may reach another device: no remote copies, remote signals or barrier semaphores. Data moves between devices by JAX's collectives and lax.ppermute only.
A program may use at most 128 MiB of HBM per device.

v0:
```python
import math
import jax
import jax.numpy as jnp
from jax import lax
from jax.sharding import PartitionSpec as P

ITERS = 2
regularizer_strength = 0.05


def shifted(x, axis, by):
    length = lax.axis_size(axis)
    return lax.ppermute(x, axis, [(i, (i + by) % length) for i in range(length)])


def normalize(values):
    floats = values.astype(jnp.float32)
    return (floats / jnp.sqrt(jnp.sum(floats * floats, axis=1, keepdims=True) + 1e-06)).astype(
        jnp.bfloat16
    )


def shards(source, target, pair_source, pair_target, pair_count):
    constituent_entries = lax.axis_size("member")
    cells_per_tile = target.shape[0]
    latent_width = target.shape[1]
    tiles_here = source.shape[0] // cells_per_tile
    unit_source = normalize(source).reshape(tiles_here, cells_per_tile, latent_width)
    unit_target = normalize(target)
    next_target = shifted(unit_target, "group", -1)
    own_window, next_window = (
        lax.all_gather(unit_target, "member", axis=0, tiled=True),
        lax.all_gather(next_target, "member", axis=0, tiled=True),
    )
    window = jnp.concatenate([own_window, next_window], 0).reshape(
        2 * constituent_entries, cells_per_tile, latent_width
    )
    slot_count = pair_source.shape[1]
    block_size = math.gcd(slot_count, 16)
    block_count = slot_count // block_size
    source_slots = pair_source[0]
    window_slots = pair_target[0]
    surviving_indicator = (jnp.arange(slot_count, dtype=jnp.int32) < pair_count[0]).astype(
        jnp.float32
    )
    block_ids = jnp.arange(block_count, dtype=jnp.int32)
    source_blocks = source_slots.reshape(block_count, block_size)
    window_blocks = window_slots.reshape(block_count, block_size)
    keep_blocks = surviving_indicator.reshape(block_count, block_size)
    pick_source = (
        source_slots[:, None] == jnp.arange(tiles_here, dtype=jnp.int32)[None, :]
    ).astype(jnp.float32)
    pick_window = (
        window_slots[:, None] == jnp.arange(2 * constituent_entries, dtype=jnp.int32)[None, :]
    ).astype(jnp.float32)

    def kernels(block_items):
        source_ids, frame_labels, retained_portion = block_items
        own_rows = unit_source[source_ids]
        partners = window[frame_labels]
        similarity_logits = jnp.einsum(
            "pid,pjd->pij", own_rows, partners, preferred_element_type=jnp.float32
        )
        return (
            jnp.exp(similarity_logits / regularizer_strength)
            / cells_per_tile
            * retained_portion[:, None, None]
        ).astype(jnp.bfloat16)

    cached = lax.map(kernels, (source_blocks, window_blocks, keep_blocks))

    def kernel_block(block_items):
        block_index, source_ids, frame_labels, retained_portion = block_items
        return lax.dynamic_index_in_dim(cached, block_index, 0, keepdims=False)

    scale_window = jnp.ones((2 * constituent_entries, cells_per_tile), jnp.float32)
    scale_source = jnp.ones((tiles_here, cells_per_tile), jnp.float32)
    scale_target = jnp.ones((cells_per_tile,), jnp.float32)
    block_inputs = (block_ids, source_blocks, window_blocks, keep_blocks)
    for sweep_number in range(ITERS):

        def row_block(block_items, scale_window=scale_window):
            boltzmann_factor_patches = kernel_block(block_items)
            weights = scale_window[block_items[2]]
            return jnp.sum(
                boltzmann_factor_patches.astype(jnp.float32) * weights[:, None, :], axis=2
            )

        row_parts = lax.map(row_block, block_inputs).reshape(slot_count, cells_per_tile)
        row_sums = jnp.einsum("ps,pi->si", pick_source, row_parts, precision=lax.Precision.HIGHEST)
        scale_source = 1.0 / row_sums

        def column_block(block_items, scale_source=scale_source):
            boltzmann_factor_patches = kernel_block(block_items)
            weights = scale_source[block_items[1]]
            return jnp.sum(
                boltzmann_factor_patches.astype(jnp.float32) * weights[:, :, None], axis=1
            )

        column_parts = lax.map(column_block, block_inputs).reshape(slot_count, cells_per_tile)
        column_terms = jnp.einsum(
            "pw,pj->wj", pick_window, column_parts, precision=lax.Precision.HIGHEST
        )
        arrived_next = shifted(column_terms[constituent_entries:], "group", 1)
        columns = lax.psum_scatter(
            column_terms[:constituent_entries] + arrived_next,
            "member",
            scatter_dimension=0,
            tiled=True,
        )[0]
        scale_target = float(tiles_here) / columns
        if sweep_number + 1 < ITERS:
            neighbour_scale = shifted(scale_target[None], "group", -1)
            range_scale, next_scale = (
                lax.all_gather(scale_target[None], "member", axis=0, tiled=True),
                lax.all_gather(neighbour_scale, "member", axis=0, tiled=True),
            )
            scale_window = jnp.concatenate([range_scale, next_scale], 0)
    return (jnp.log(scale_source).reshape(tiles_here * cells_per_tile), jnp.log(scale_target))


def solution(mesh):
    placed = (
        P(("group", "member"), None),
        P(("group", "member"), None),
        P(("group", "member"), None),
        P(("group", "member"), None),
        P(("group", "member")),
    )
    return jax.shard_map(
        shards,
        mesh=mesh,
        in_specs=placed,
        out_specs=(P(("group", "member")), P(("group", "member"))),
        check_vma=False,
    )
```

profile of v0, /device:TPU:0, one launch (start us, length us, event | category | flops | bytes accessed | tf_op | source)
XLA Modules:
  0.0 186.2 jit_solution(13188330610118061224)
XLA Ops:
  10.0 5.1 %collective-permute-start = (bf16[256,256]{1,0:T(8,128)(2,1)}, bf16[256,256]{1,0:T(8,128)(2,1)S(1)}, u32[]{:S(2)}, u32[]{:S(2)}) collective-permute-start(bf16[256,256]{1,0:T(8,128)(2,1)} %fusion.21), channel_id=1, source_target_pairs={{0,24},{8,0},{16,8},{24,16},{1,25},{9,1},{17,9},{25,17},{2,26},{10... | collective-permute-start | bytes 393224 | tf_op jit(solution)/shard_map/ppermute | solution.py:13
  15.1 3.1 %collective-permute-done = bf16[256,256]{1,0:T(8,128)(2,1)S(1)} collective-permute-done((bf16[256,256]{1,0:T(8,128)(2,1)}, bf16[256,256]{1,0:T(8,128)(2,1)S(1)}, u32[]{:S(2)}, u32[]{:S(2)}) %collective-permute-start) | collective-permute-done | bytes 131104 | tf_op jit(solution)/shard_map/ppermute | solution.py:13
  25.4 10.8 %all-gather.5.cloned.1.call-done = bf16[2048,256]{1,0:T(8,128)(2,1)} async-done(((bf16[256,256]{1,0:T(8,128)(2,1)}), bf16[2048,256]{1,0:T(8,128)(2,1)}) %all-gather.5.cloned.1.call-update) | async-done | bytes 1048592 | tf_op jit(solution)/shard_map/all_gather | solution.py:32
  36.2 25.3 %all-gather.7.cloned.1.call-done = bf16[2048,256]{1,0:T(8,128)(2,1)} async-done(((bf16[256,256]{1,0:T(8,128)(2,1)}), bf16[2048,256]{1,0:T(8,128)(2,1)}) %all-gather.7.cloned.1.call-update) | async-done | bytes 1048592 | tf_op jit(solution)/shard_map/all_gather | solution.py:33
  63.1 16.9 %while.50 = (s32[]{:T(128)}, bf16[2,16,256,256]{3,2,1,0:T(8,128)(2,1)}, s32[2,16]{1,0:T(2,128)S(1)}, bf16[4,256,256]{2,1,0:T(8,128)(2,1)S(1)}, s32[2,16]{1,0:T(2...) while((s32[]{:T(128)}, bf16[2,16,256,256]{3,2,1,0:T(8,128)(2,1)}, ...), condition=%wide.region_3.4_spmd, body=%wide.region_2.3_spmd.sunk | while | flops 540018816 | bytes 14689565 | solution.py:70
  63.2 2.0 %gather_fusion = bf16[16,256,256]{2,1,0:T(8,128)(2,1)} fusion(bf16[4,256,256]{2,1,0:T(8,128)(2,1)S(1)} %get-tuple-element.437, s32[1024]{0:T(1024)S(1)} %pad_clamp_fusion.12), kind=kCustom, calls=%fused_computation.clone.1 | custom fusion | bytes 4194368 | tf_op jit(solution)/shard_map/while/body/eval_jaxpr/gather | solution.py:59
  65.2 2.0 %gather_fusion.1 = bf16[16,256,256]{2,1,0:T(8,128)(2,1)} fusion(bf16[16,256,256]{2,1,0:T(8,128)(2,1)S(1)} %get-tuple-element.439, s32[1024]{0:T(1024)S(1)} %pad_clamp_fusion.13), kind=kCustom, calls=%fused_computation.1.clone.1 | custom fusion | bytes 4194368 | tf_op jit(solution)/shard_map/while/body/eval_jaxpr/gather | solution.py:60
  67.2 4.4 %bitcast_dynamic-update-slice_fusion.10 = bf16[2,16,256,256]{3,2,1,0:T(8,128)(2,1)} fusion(bf16[2,16,256,256]{3,2,1,0:T(8,128)(2,1)} %get-tuple-element.427, s32[]{:T(128)} %get-tuple-element.426, f32[16]{0:T(128)S(1)} %fusion.50, bf16[16,256,256]{2,1,0:T(8,128)(2,1)} %gather_fusion, bf16[16,256,256]{2,1,0:T(8,128)(2,1)} %gather_fusion.1), kind=kOutput, calls=%fused_computation.7.clone.1 | convolution fusion | flops 540016640 | bytes 6292032 | tf_op jit(solution)/shard_map/while/body/eval_jaxpr/pid,pjd->pij/dot_general | solution.py:61
  73.7 2.0 %gather_fusion.1 = bf16[16,256,256]{2,1,0:T(8,128)(2,1)} fusion(bf16[16,256,256]{2,1,0:T(8,128)(2,1)S(1)} %get-tuple-element.439, s32[1024]{0:T(1024)S(1)} %pad_clamp_fusion.13), kind=kCustom, calls=%fused_computation.1.clone.1 | custom fusion | bytes 4194368 | tf_op jit(solution)/shard_map/while/body/eval_jaxpr/gather | solution.py:60
  75.7 4.3 %bitcast_dynamic-update-slice_fusion.10 = bf16[2,16,256,256]{3,2,1,0:T(8,128)(2,1)} fusion(bf16[2,16,256,256]{3,2,1,0:T(8,128)(2,1)} %get-tuple-element.427, s32[]{:T(128)} %get-tuple-element.426, f32[16]{0:T(128)S(1)} %fusion.50, bf16[16,256,256]{2,1,0:T(8,128)(2,1)} %gather_fusion, bf16[16,256,256]{2,1,0:T(8,128)(2,1)} %gather_fusion.1), kind=kOutput, calls=%fused_computation.7.clone.1 | convolution fusion | flops 540016640 | bytes 6292032 | tf_op jit(solution)/shard_map/while/body/eval_jaxpr/pid,pjd->pij/dot_general | solution.py:61
  80.1 10.6 %while.51 = (s32[]{:T(128)}, f32[2,16,256]{2,1,0:T(8,128)S(1)}, s32[2]{0:T(128)S(1)}, bf16[2,16,256,256]{3,2,1,0:T(8,128)(2,1)}, s32[2,16]{1,0:T(2,128)S(1)}, /*index=5*/s32[]{:T(128)}, f32[]{:T(128)}, s32[]{:T(128)}, s32[]{:T(128)}) while((s32[]{:T(128)}, f32[2,16,256]{2,1,0:T(8,128)S(1)}, s32[2]{0:T(128)S(1)}, ...), condition=%wide.region_6.7_spmd, body=%wide.region_4.6_spmd.sunk | while | flops 3142709 | bytes 2216347 | solution.py:89
  83.2 2.2 %fusion.53 = f32[16,256]{1,0:T(8,128)S(1)} fusion(f32[16,256]{1,0:T(8,128)S(1)} %gather_fusion.2, bf16[2,16,256,256]{3,2,1,0:T(8,128)(2,1)} %get-tuple-element.463, s32[]{:T(128)S(6)} %select_n.102), kind=kLoop, calls=%fused_computation.22.clone.1 | loop fusion | flops 3141632 | bytes 2129924 | tf_op jit(solution)/shard_map/while/body/eval_jaxpr/reduce_sum | solution.py:85
  88.5 2.2 %fusion.53 = f32[16,256]{1,0:T(8,128)S(1)} fusion(f32[16,256]{1,0:T(8,128)S(1)} %gather_fusion.2, bf16[2,16,256,256]{3,2,1,0:T(8,128)(2,1)} %get-tuple-element.463, s32[]{:T(128)S(6)} %select_n.102), kind=kLoop, calls=%fused_computation.22.clone.1 | loop fusion | flops 3141632 | bytes 2129924 | tf_op jit(solution)/shard_map/while/body/eval_jaxpr/reduce_sum | solution.py:85
  91.0 10.3 %while.52 = (s32[]{:T(128)}, f32[2,16,256]{2,1,0:T(8,128)S(1)}, s32[2]{0:T(128)S(1)}, bf16[2,16,256,256]{3,2,1,0:T(8,128)(2,1)}, s32[2,16]{1,0:T(2,128)S(1)}, /*...) while((s32[]{:T(128)}, f32[2,16,256]{2,1,0:T(8,128)S(1)}, s32[2]{0:T(128)S(1)}, ...), condition=%wide.region_9.10_spmd, body=%wide.region_7.9_spmd.sunk | while | flops 3142709 | bytes 2199959 | solution.py:100
  103.7 3.4 %collective-permute-done.1 = f32[8,256]{1,0:T(8,128)S(1)} collective-permute-done((f32[8,256]{1,0:T(8,128)S(1)}, f32[8,256]{1,0:T(8,128)S(1)}, u32[]{:S(2)}, u32[]{:S(2)}) %collective-permute-start.1) | collective-permute-done | bytes 8224 | tf_op jit(solution)/shard_map/ppermute | solution.py:13
  107.1 12.2 %all-reduce = f32[8,256]{1,0:T(8,128)S(1)} all-reduce(f32[8,256]{1,0:T(8,128)S(1)} %slice_add_fusion.1), channel_id=2, replica_groups=mesh['group'=4,'member'=8] {'member'}, use_global_device_ids=true, to_apply=%region_10.11.clone | all-reduce | flops 2048 | bytes 16384
  122.1 8.9 %all-gather = f32[8,1,256]{2,1,0:T(1,128)S(1)} all-gather(f32[1,1,256]{2,1,0:T(1,128)S(1)} %fusion.35), channel_id=1, replica_groups=mesh['group'=4,'member'=8] {'member'}, dimensions={0}, use_global_device_ids=true | all-gather | bytes 9216 | tf_op jit(solution)/shard_map/all_gather | solution.py:115
  131.0 8.0 %all-gather.1 = f32[8,1,256]{2,1,0:T(1,128)S(1)} all-gather(f32[1,1,256]{2,1,0:T(1,128)S(1)} %bitcast.167), channel_id=1, replica_groups=mesh['group'=4,'member'=8] {'member'}, dimensions={0}, use_global_device_ids=true | all-gather | bytes 9216 | tf_op jit(solution)/shard_map/all_gather | solution.py:116
  139.0 10.6 %while.53 = (s32[]{:T(128)}, f32[2,16,256]{2,1,0:T(8,128)S(1)}, s32[2]{0:T(128)S(1)}, bf16[2,16,256,256]{3,2,1,0:T(8,128)(2,1)}, s32[2,16]{1,0:T(2,128)S(1)}, /*...) while((s32[]{:T(128)}, f32[2,16,256]{2,1,0:T(8,128)S(1)}, s32[2]{0:T(128)S(1)}, ...), condition=%wide.region_13.14_spmd, body=%wide.region_11.13_spmd.sunk | while | flops 3142709 | bytes 2199959 | solution.py:89
  142.0 2.2 %fusion.57 = f32[16,256]{1,0:T(8,128)S(1)} fusion(f32[16,256]{1,0:T(8,128)S(1)} %gather_fusion.4, bf16[2,16,256,256]{3,2,1,0:T(8,128)(2,1)} %get-tuple-element.517, s32[]{:T(128)S(6)} %select_n.106), kind=kLoop, calls=%fused_computation.38.clone.1 | loop fusion | flops 3141632 | bytes 2129924 | tf_op jit(solution)/shard_map/while/body/eval_jaxpr/reduce_sum | solution.py:85
  147.3 2.2 %fusion.57 = f32[16,256]{1,0:T(8,128)S(1)} fusion(f32[16,256]{1,0:T(8,128)S(1)} %gather_fusion.4, bf16[2,16,256,256]{3,2,1,0:T(8,128)(2,1)} %get-tuple-element.517, s32[]{:T(128)S(6)} %select_n.106), kind=kLoop, calls=%fused_computation.38.clone.1 | loop fusion | flops 3141632 | bytes 2129924 | tf_op jit(solution)/shard_map/while/body/eval_jaxpr/reduce_sum | solution.py:85
  149.8 10.3 %while.54 = (s32[]{:T(128)}, f32[2,16,256]{2,1,0:T(8,128)S(1)}, s32[2]{0:T(128)S(1)}, bf16[2,16,256,256]{3,2,1,0:T(8,128)(2,1)}, s32[2,16]{1,0:T(2,128)S(1)}, /*...) while((s32[]{:T(128)}, f32[2,16,256]{2,1,0:T(8,128)S(1)}, s32[2]{0:T(128)S(1)}, ...), condition=%wide.region_16.17_spmd, body=%wide.region_14.16_spmd.sunk | while | flops 3142709 | bytes 2199959 | solution.py:100
  161.5 4.3 %collective-permute-done.3 = f32[8,256]{1,0:T(8,128)S(1)} collective-permute-done((f32[8,256]{1,0:T(8,128)S(1)}, f32[8,256]{1,0:T(8,128)S(1)}, u32[]{:S(2)}, u32[]{:S(2)}) %collective-permute-start.3) | collective-permute-done | bytes 8224 | tf_op jit(solution)/shard_map/ppermute | solution.py:13
  165.9 12.3 %all-reduce.1 = f32[8,256]{1,0:T(8,128)S(1)} all-reduce(f32[8,256]{1,0:T(8,128)S(1)} %slice_add_fusion), channel_id=3, replica_groups=mesh['group'=4,'member'=8] {'member'}, use_global_device_ids=true, to_apply=%region_17.18.clone | all-reduce | flops 2048 | bytes 16384
  (110 shorter events, 38.8 us)
Async XLA Ops:
  7.2 29.0 %all-gather.5.cloned.1.call-start = ((), (), s32[]{:S(2)}) async-start(), calls=%async_computation | async-start | bytes 1179648 | tf_op jit(solution)/shard_map/all_gather | solution.py:32
  9.9 51.5 %all-gather.7.cloned.1.call-start = ((), (), s32[]{:S(2)}) async-start(), calls=%async_computation.1 | async-start | bytes 1179648 | tf_op jit(solution)/shard_map/all_gather | solution.py:33
  10.0 8.2 %collective-permute-start = (bf16[256,256]{1,0:T(8,128)(2,1)}, bf16[256,256]{1,0:T(8,128)(2,1)S(1)}, u32[]{:S(2)}, u32[]{:S(2)}) collective-permute-start(bf16[256,256]{1,0:T(8,128)(2,1)} %fusion.21), channel_id=1, source_target_pairs={{0,24},{8,0},{16,8},{24,16},{1,25},{9,1},{17,9},{25,17},{2,26},{10... | collective-permute-start | bytes 393224 | tf_op jit(solution)/shard_map/ppermute | solution.py:13
  18.2 0.7 copy-start
  80.1 10.7 %copy-start.1 = (s32[1,32]{1,0:T(1,128)S(1)}, s32[1,32]{1,0:T(1,128)}, u32[]{:S(2)}) copy-start(s32[1,32]{1,0:T(1,128)} %param.17) | copy-start | bytes 388
  91.0 10.3 %copy-start.2 = (s32[1,32]{1,0:T(1,128)S(1)}, s32[1,32]{1,0:T(1,128)}, u32[]{:S(2)}) copy-start(s32[1,32]{1,0:T(1,128)} %param.18) | copy-start | bytes 388
  91.0 12.1 %copy-start.3 = (u32[32]{0:T(128)S(1)}, u32[32]{0:T(128)}, u32[]{:S(2)}) copy-start(u32[32]{0:T(128)} %constant.109) | copy-start | bytes 388
  101.6 5.5 %collective-permute-start.1 = (f32[8,256]{1,0:T(8,128)S(1)}, f32[8,256]{1,0:T(8,128)S(1)}, u32[]{:S(2)}, u32[]{:S(2)}) collective-permute-start(f32[8,256]{1,0:T(8,128)S(1)} %slice.29), channel_id=1, source_target_pairs={{0,8},{8,16},{16,24},{24,0},{1,9},{9,17},{17,25},{25,1},{2,10},{10... | collective-permute-start | bytes 24584 | tf_op jit(solution)/shard_map/ppermute | solution.py:13
  120.5 10.5 %collective-permute-start.2 = (f32[1,256]{1,0:T(1,128)S(1)}, f32[1,256]{1,0:T(1,128)S(1)}, u32[]{:S(2)}, u32[]{:S(2)}) collective-permute-start(f32[1,256]{1,0:T(1,128)S(1)} %dynamic-slice_divide_fusion.1), channel_id=1, source_target_pairs={{0,24},{8,0},{16,8},{24,16},{1,25},{9,1},{17,9},{25,17},{2,26},{10... | collective-permute-start | bytes 3080 | tf_op jit(solution)/shard_map/ppermute | solution.py:13
  160.4 5.5 %collective-permute-start.3 = (f32[8,256]{1,0:T(8,128)S(1)}, f32[8,256]{1,0:T(8,128)S(1)}, u32[]{:S(2)}, u32[]{:S(2)}) collective-permute-start(f32[8,256]{1,0:T(8,128)S(1)} %slice.31), channel_id=1, source_target_pairs={{0,8},{8,16},{16,24},{24,0},{1,9},{9,17},{17,25},{25,1},{2,10},{10... | collective-permute-start | bytes 24584 | tf_op jit(solution)/shard_map/ppermute | solution.py:13
Sparse Core Ops, SparseCore 0:
  10.0 26.0 all-gather.4
  38.1 23.3 all-gather.6
where the time goes:
time: 187 us; the launch traced here: 186 us
  waiting for transfers between devices  46.9 us (25%)
  blocking collectives  41.3 us (22%)
  other arithmetic  28.8 us (15%)
  local copies, waits for them, and re-layouts  20.1 us (11%)
  loops' own time  15.6 us (8%)
  between operations  14.9 us (8%)
  matrix products  9.78 us (5%)
  starting transfers between devices  8.88 us (5%)
    all_gather x1, waiting for transfers between devices, shards(): lax.all_gather(next_target, 'member', axis=0, tiled=True)  25.3 us
    unnamed x2, blocking collectives  24.5 us
    all_gather x1, waiting for transfers between devices, shards(): lax.all_gather(unit_target, 'member', axis=0, tiled=True)  10.8 us
    ppermute x4, waiting for transfers between devices, shifted(): lax.ppermute(x, axis, [(i, (i + by) % length) for i in range(length)])  10.8 us
    all_gather x1, blocking collectives, shards(): lax.all_gather(scale_target[None], 'member', axis=0, tiled=True)  8.88 us
    reduce_sum x4, other arithmetic, row_block(): jnp.sum(boltzmann_factor_patches.astype(jnp.float32) * weights[:, None, :...  8.85 us
    ppermute x4, starting transfers between devices, shifted(): lax.ppermute(x, axis, [(i, (i + by) % length) for i in range(length)])  8.8 us
    dot_general x2, matrix products, kernels(): jnp.einsum('pid,pjd->pij', own_rows, partners, preferred_element_type=jnp...  8.75 us
  transfers between devices with their start and end apart: 6, of which 5 were waited for; matrix products, arithmetic and copies ran while one was open for 4% of the time, Pallas kernels for 0%

commit v1 on v0

--- a/solution.py
+++ b/solution.py
@@ -28,9 +28,21 @@
     unit_source = normalize(source).reshape(tiles_here, cells_per_tile, latent_width)
     unit_target = normalize(target)
     next_target = shifted(unit_target, "group", -1)
+
+    def heaps_scan(x_part, mesh_dim):
+        y1, oldest, block_now = (lax.axis_size(mesh_dim), lax.axis_index(mesh_dim), x_part.shape[0])
+        carry_in, kept_arr = (x_part, 1)
+        while kept_arr < y1:
+            tray = []
+            for idx in range(y1):
+                tray.append((idx, (idx - kept_arr) % y1))
+            carry_in = jnp.concatenate([carry_in, lax.ppermute(carry_in, mesh_dim, tray)], axis=0)
+            kept_arr = 2 * kept_arr
+        return jnp.roll(carry_in, oldest * block_now, 0)
+
     own_window, next_window = (
         lax.all_gather(unit_target, "member", axis=0, tiled=True),
-        lax.all_gather(next_target, "member", axis=0, tiled=True),
+        heaps_scan(next_target, "member"),
     )
     window = jnp.concatenate([own_window, next_window], 0).reshape(
         2 * constituent_entries, cells_per_tile, latent_width

time: 187 us -> 176 us (0.941)
  waiting for transfers between devices: 46.9 us -> 35.8 us
  other arithmetic: 28.8 us -> 25.9 us
    all_gather x1 -> x0, waiting for transfers between devices: 25.3 us -> none  [shards(): lax.all_gather(next_target, 'member', axis=0, tiled=True)]
    ppermute x0 -> x3, waiting for transfers between devices: none -> 23.1 us  [heaps_scan(): lax.ppermute(carry_in, mesh_dim, tray)]
    all_gather x1, waiting for transfers between devices: 10.8 us -> 0.01 us  [shards(): lax.all_gather(unit_target, 'member', axis=0, tiled=True)]
    ppermute x0 -> x3, starting transfers between devices: none -> 2.57 us  [heaps_scan(): lax.ppermute(carry_in, mesh_dim, tray)]
    ppermute x4, waiting for transfers between devices: 10.8 us -> 12.8 us  [shifted(): lax.ppermute(x, axis, [(i, (i + by) % length) for i in range(length)])]
  transfers between devices with their start and end apart: 6 -> 8, of which waited for: 5 -> 6; matrix products, arithmetic and copies ran while one was open for 4% -> 3% of each run, Pallas kernels for 0% -> 0%
where the time goes in v1:
time: 176 us; the launch traced here: 175 us
  blocking collectives  42.7 us (24%)
  waiting for transfers between devices  35.8 us (20%)
  other arithmetic  25.9 us (15%)
  local copies, waits for them, and re-layouts  20.7 us (12%)
  loops' own time  15.6 us (9%)
  between operations  15 us (9%)
  starting transfers between devices  9.93 us (6%)
  matrix products  9.78 us (6%)
    unnamed x2, blocking collectives  25.8 us
    ppermute x3, waiting for transfers between devices, heaps_scan(): lax.ppermute(carry_in, mesh_dim, tray)  23.1 us
    ppermute x4, waiting for transfers between devices, shifted(): lax.ppermute(x, axis, [(i, (i + by) % length) for i in range(length)])  12.8 us
    all_gather x1, blocking collectives, shards(): lax.all_gather(neighbour_scale, 'member', axis=0, tiled=True)  8.98 us
    reduce_sum x4, other arithmetic, row_block(): jnp.sum(boltzmann_factor_patches.astype(jnp.float32) * weights[:, None, :...  8.85 us
    dot_general x2, matrix products, kernels(): jnp.einsum('pid,pjd->pij', own_rows, partners, preferred_element_type=jnp...  8.75 us
    another operation x2, loops' own time, shards(): lax.map(column_block, block_inputs).reshape(slot_count, cells_per_tile)  7.97 us
    all_gather x1, blocking collectives, shards(): lax.all_gather(scale_target[None], 'member', axis=0, tiled=True)  7.86 us
  transfers between devices with their start and end apart: 8, of which 6 were waited for; matrix products, arithmetic and copies ran while one was open for 3% of the time, Pallas kernels for 0%

profile of v1, /device:TPU:0, one launch (start us, length us, event | category | flops | bytes accessed | tf_op | source)
XLA Modules:
  0.0 175.4 jit_solution(1192940600028745861)
XLA Ops:
  9.3 5.1 %collective-permute-start = (bf16[256,256]{1,0:T(8,128)(2,1)S(1)}, bf16[256,256]{1,0:T(8,128)(2,1)S(1)}, u32[]{:S(2)}, u32[]{:S(2)}) collective-permute-start(bf16[256,256]{1,0:T(8,128)(2,1)S(1)} %fusion.21), channel_id=1, source_target_pairs={{0,24},{8,0},{16,8},{24,16},{1,25},{9,1},{17,9},{25,17},{2,26},{10... | collective-permute-start | bytes 393224 | tf_op jit(solution)/shard_map/ppermute | solution.py:13
  14.5 2.8 %collective-permute-done = bf16[256,256]{1,0:T(8,128)(2,1)S(1)} collective-permute-done((bf16[256,256]{1,0:T(8,128)(2,1)S(1)}, bf16[256,256]{1,0:T(8,128)(2,1)S(1)}, u32[]{:S(2)}, u32[]{:S(2)}) %collective-permute-start) | collective-permute-done | bytes 131104 | tf_op jit(solution)/shard_map/ppermute | solution.py:13
  18.3 2.5 %collective-permute-done.1 = bf16[256,256]{1,0:T(8,128)(2,1)S(1)} collective-permute-done((bf16[256,256]{1,0:T(8,128)(2,1)S(1)}, bf16[256,256]{1,0:T(8,128)(2,1)S(1)}, u32[]{:S(2)}, u32[]{:S(2)}) %collective-permute-start.1) | collective-permute-done | bytes 131104 | tf_op jit(solution)/shard_map/ppermute | solution.py:39
  23.6 6.7 %collective-permute-done.2 = bf16[512,256]{1,0:T(8,128)(2,1)S(1)} collective-permute-done((bf16[512,256]{1,0:T(8,128)(2,1)S(1)}, bf16[512,256]{1,0:T(8,128)(2,1)S(1)}, u32[]{:S(2)}, u32[]{:S(2)}) %collective-permute-start.2) | collective-permute-done | bytes 262176 | tf_op jit(solution)/shard_map/ppermute | solution.py:39
  33.4 13.9 %collective-permute-done.3 = bf16[1024,256]{1,0:T(8,128)(2,1)S(1)} collective-permute-done((bf16[1024,256]{1,0:T(8,128)(2,1)S(1)}, bf16[1024,256]{1,0:T(8,128)(2,1)S(1)}, u32[]{:S(2)}, u32[]{:S(2)}) %collective-permute-start.3) | collective-permute-done | bytes 524320 | tf_op jit(solution)/shard_map/ppermute | solution.py:39
  50.2 16.9 %while.50 = (s32[]{:T(128)}, bf16[2,16,256,256]{3,2,1,0:T(8,128)(2,1)}, s32[2,16]{1,0:T(2,128)S(1)}, bf16[4,256,256]{2,1,0:T(8,128)(2,1)S(1)}, s32[2,16]{1,0:T(2...) while((s32[]{:T(128)}, bf16[2,16,256,256]{3,2,1,0:T(8,128)(2,1)}, ...), condition=%wide.region_3.4_spmd, body=%wide.region_2.3_spmd.sunk | while | flops 540018816 | bytes 14689565 | solution.py:82
  52.2 2.0 %gather_fusion.1 = bf16[16,256,256]{2,1,0:T(8,128)(2,1)} fusion(bf16[16,256,256]{2,1,0:T(8,128)(2,1)S(1)} %get-tuple-element.439, s32[1024]{0:T(1024)S(1)} %pad_clamp_fusion.13), kind=kCustom, calls=%fused_computation.1.clone.1 | custom fusion | bytes 4194368 | tf_op jit(solution)/shard_map/while/body/eval_jaxpr/gather | solution.py:72
  54.3 4.4 %bitcast_dynamic-update-slice_fusion.10 = bf16[2,16,256,256]{3,2,1,0:T(8,128)(2,1)} fusion(bf16[2,16,256,256]{3,2,1,0:T(8,128)(2,1)} %get-tuple-element.427, s32[]{:T(128)} %get-tuple-element.426, f32[16]{0:T(128)S(1)} %fusion.50, bf16[16,256,256]{2,1,0:T(8,128)(2,1)} %gather_fusion, bf16[16,256,256]{2,1,0:T(8,128)(2,1)} %gather_fusion.1), kind=kOutput, calls=%fused_computation.7.clone.1 | convolution fusion | flops 540016640 | bytes 6292032 | tf_op jit(solution)/shard_map/while/body/eval_jaxpr/pid,pjd->pij/dot_general | solution.py:73
  60.7 2.0 %gather_fusion.1 = bf16[16,256,256]{2,1,0:T(8,128)(2,1)} fusion(bf16[16,256,256]{2,1,0:T(8,128)(2,1)S(1)} %get-tuple-element.439, s32[1024]{0:T(1024)S(1)} %pad_clamp_fusion.13), kind=kCustom, calls=%fused_computation.1.clone.1 | custom fusion | bytes 4194368 | tf_op jit(solution)/shard_map/while/body/eval_jaxpr/gather | solution.py:72
  62.7 4.3 %bitcast_dynamic-update-slice_fusion.10 = bf16[2,16,256,256]{3,2,1,0:T(8,128)(2,1)} fusion(bf16[2,16,256,256]{3,2,1,0:T(8,128)(2,1)} %get-tuple-element.427, s32[]{:T(128)} %get-tuple-element.426, f32[16]{0:T(128)S(1)} %fusion.50, bf16[16,256,256]{2,1,0:T(8,128)(2,1)} %gather_fusion, bf16[16,256,256]{2,1,0:T(8,128)(2,1)} %gather_fusion.1), kind=kOutput, calls=%fused_computation.7.clone.1 | convolution fusion | flops 540016640 | bytes 6292032 | tf_op jit(solution)/shard_map/while/body/eval_jaxpr/pid,pjd->pij/dot_general | solution.py:73
  67.1 10.6 %while.51 = (s32[]{:T(128)}, f32[2,16,256]{2,1,0:T(8,128)S(1)}, s32[2]{0:T(128)S(1)}, bf16[2,16,256,256]{3,2,1,0:T(8,128)(2,1)}, s32[2,16]{1,0:T(2,128)S(1)}, /*index=5*/s32[]{:T(128)}, f32[]{:T(128)}, s32[]{:T(128)}, s32[]{:T(128)}) while((s32[]{:T(128)}, f32[2,16,256]{2,1,0:T(8,128)S(1)}, s32[2]{0:T(128)S(1)}, ...), condition=%wide.region_6.7_spmd, body=%wide.region_4.6_spmd.sunk | while | flops 3142709 | bytes 2216347 | solution.py:101
  70.2 2.2 %fusion.53 = f32[16,256]{1,0:T(8,128)S(1)} fusion(f32[16,256]{1,0:T(8,128)S(1)} %gather_fusion.2, bf16[2,16,256,256]{3,2,1,0:T(8,128)(2,1)} %get-tuple-element.463, s32[]{:T(128)S(6)} %select_n.117), kind=kLoop, calls=%fused_computation.22.clone.1 | loop fusion | flops 3141632 | bytes 2129924 | tf_op jit(solution)/shard_map/while/body/eval_jaxpr/reduce_sum | solution.py:97
  75.5 2.2 %fusion.53 = f32[16,256]{1,0:T(8,128)S(1)} fusion(f32[16,256]{1,0:T(8,128)S(1)} %gather_fusion.2, bf16[2,16,256,256]{3,2,1,0:T(8,128)(2,1)} %get-tuple-element.463, s32[]{:T(128)S(6)} %select_n.117), kind=kLoop, calls=%fused_computation.22.clone.1 | loop fusion | flops 3141632 | bytes 2129924 | tf_op jit(solution)/shard_map/while/body/eval_jaxpr/reduce_sum | solution.py:97
  78.0 10.3 %while.52 = (s32[]{:T(128)}, f32[2,16,256]{2,1,0:T(8,128)S(1)}, s32[2]{0:T(128)S(1)}, bf16[2,16,256,256]{3,2,1,0:T(8,128)(2,1)}, s32[2,16]{1,0:T(2,128)S(1)}, /*...) while((s32[]{:T(128)}, f32[2,16,256]{2,1,0:T(8,128)S(1)}, s32[2]{0:T(128)S(1)}, ...), condition=%wide.region_9.10_spmd, body=%wide.region_7.9_spmd.sunk | while | flops 3142709 | bytes 2199959 | solution.py:112
  89.2 5.4 %collective-permute-done.4 = f32[8,256]{1,0:T(8,128)S(1)} collective-permute-done((f32[8,256]{1,0:T(8,128)S(1)}, f32[8,256]{1,0:T(8,128)S(1)}, u32[]{:S(2)}, u32[]{:S(2)}) %collective-permute-start.4) | collective-permute-done | bytes 8224 | tf_op jit(solution)/shard_map/ppermute | solution.py:13
  94.7 13.6 %all-reduce = f32[8,256]{1,0:T(8,128)S(1)} all-reduce(f32[8,256]{1,0:T(8,128)S(1)} %slice_add_fusion.1), channel_id=2, replica_groups=mesh['group'=4,'member'=8] {'member'}, use_global_device_ids=true, to_apply=%region_10.11.clone | all-reduce | flops 2048 | bytes 16384
  111.3 7.9 %all-gather = f32[8,1,256]{2,1,0:T(1,128)S(1)} all-gather(f32[1,1,256]{2,1,0:T(1,128)S(1)} %fusion.35), channel_id=1, replica_groups=mesh['group'=4,'member'=8] {'member'}, dimensions={0}, use_global_device_ids=true | all-gather | bytes 9216 | tf_op jit(solution)/shard_map/all_gather | solution.py:127
  119.1 9.0 %all-gather.1 = f32[8,1,256]{2,1,0:T(1,128)S(1)} all-gather(f32[1,1,256]{2,1,0:T(1,128)S(1)} %bitcast.167), channel_id=1, replica_groups=mesh['group'=4,'member'=8] {'member'}, dimensions={0}, use_global_device_ids=true | all-gather | bytes 9216 | tf_op jit(solution)/shard_map/all_gather | solution.py:128
  128.1 10.6 %while.53 = (s32[]{:T(128)}, f32[2,16,256]{2,1,0:T(8,128)S(1)}, s32[2]{0:T(128)S(1)}, bf16[2,16,256,256]{3,2,1,0:T(8,128)(2,1)}, s32[2,16]{1,0:T(2,128)S(1)}, /*...) while((s32[]{:T(128)}, f32[2,16,256]{2,1,0:T(8,128)S(1)}, s32[2]{0:T(128)S(1)}, ...), condition=%wide.region_13.14_spmd, body=%wide.region_11.13_spmd.sunk | while | flops 3142709 | bytes 2199959 | solution.py:101
  131.2 2.2 %fusion.57 = f32[16,256]{1,0:T(8,128)S(1)} fusion(f32[16,256]{1,0:T(8,128)S(1)} %gather_fusion.4, bf16[2,16,256,256]{3,2,1,0:T(8,128)(2,1)} %get-tuple-element.517, s32[]{:T(128)S(6)} %select_n.121), kind=kLoop, calls=%fused_computation.38.clone.1 | loop fusion | flops 3141632 | bytes 2129924 | tf_op jit(solution)/shard_map/while/body/eval_jaxpr/reduce_sum | solution.py:97
  136.5 2.2 %fusion.57 = f32[16,256]{1,0:T(8,128)S(1)} fusion(f32[16,256]{1,0:T(8,128)S(1)} %gather_fusion.4, bf16[2,16,256,256]{3,2,1,0:T(8,128)(2,1)} %get-tuple-element.517, s32[]{:T(128)S(6)} %select_n.121), kind=kLoop, calls=%fused_computation.38.clone.1 | loop fusion | flops 3141632 | bytes 2129924 | tf_op jit(solution)/shard_map/while/body/eval_jaxpr/reduce_sum | solution.py:97
  139.0 10.3 %while.54 = (s32[]{:T(128)}, f32[2,16,256]{2,1,0:T(8,128)S(1)}, s32[2]{0:T(128)S(1)}, bf16[2,16,256,256]{3,2,1,0:T(8,128)(2,1)}, s32[2,16]{1,0:T(2,128)S(1)}, /*...) while((s32[]{:T(128)}, f32[2,16,256]{2,1,0:T(8,128)S(1)}, s32[2]{0:T(128)S(1)}, ...), condition=%wide.region_16.17_spmd, body=%wide.region_14.16_spmd.sunk | while | flops 3142709 | bytes 2199959 | solution.py:112
  150.5 4.6 %collective-permute-done.6 = f32[8,256]{1,0:T(8,128)S(1)} collective-permute-done((f32[8,256]{1,0:T(8,128)S(1)}, f32[8,256]{1,0:T(8,128)S(1)}, u32[]{:S(2)}, u32[]{:S(2)}) %collective-permute-start.6) | collective-permute-done | bytes 8224 | tf_op jit(solution)/shard_map/ppermute | solution.py:13
  155.1 12.3 %all-reduce.1 = f32[8,256]{1,0:T(8,128)S(1)} all-reduce(f32[8,256]{1,0:T(8,128)S(1)} %slice_add_fusion), channel_id=3, replica_groups=mesh['group'=4,'member'=8] {'member'}, use_global_device_ids=true, to_apply=%region_17.18.clone | all-reduce | flops 2048 | bytes 16384
  (126 shorter events, 39.6 us)
Async XLA Ops:
  7.2 23.2 %copy-start = (bf16[1024,256]{1,0:T(8,128)(2,1)S(1)}, bf16[1024,256]{1,0:T(8,128)(2,1)}, u32[]{:S(2)}) copy-start(bf16[1024,256]{1,0:T(8,128)(2,1)} %param.15) | copy-start | bytes 1572868
  7.2 24.0 %copy-start.2 = (s32[1,32]{1,0:T(1,128)S(1)}, s32[1,32]{1,0:T(1,128)}, u32[]{:S(2)}) copy-start(s32[1,32]{1,0:T(1,128)} %param.17) | copy-start | bytes 388
  7.2 24.7 %copy-start.3 = (s32[1,32]{1,0:T(1,128)S(1)}, s32[1,32]{1,0:T(1,128)}, u32[]{:S(2)}) copy-start(s32[1,32]{1,0:T(1,128)} %param.18) | copy-start | bytes 388
  7.2 41.3 %all-gather.4.cloned.1.call-start = ((), (), s32[]{:S(2)}) async-start(), calls=%async_computation | async-start | bytes 1179648 | tf_op jit(solution)/shard_map/all_gather | solution.py:44
  9.3 8.9 %copy-start.1 = (bf16[256,256]{1,0:T(8,128)(2,1)}, bf16[256,256]{1,0:T(8,128)(2,1)S(1)}, u32[]{:S(2)}) copy-start(bf16[256,256]{1,0:T(8,128)(2,1)S(1)} %fusion.21) | copy-start | bytes 393220
  9.3 7.9 %collective-permute-start = (bf16[256,256]{1,0:T(8,128)(2,1)S(1)}, bf16[256,256]{1,0:T(8,128)(2,1)S(1)}, u32[]{:S(2)}, u32[]{:S(2)}) collective-permute-start(bf16[256,256]{1,0:T(8,128)(2,1)S(1)} %fusion.21), channel_id=1, source_target_pairs={{0,24},{8,0},{16,8},{24,16},{1,25},{9,1},{17,9},{25,17},{2,26},{10... | collective-permute-start | bytes 393224 | tf_op jit(solution)/shard_map/ppermute | solution.py:13
  17.2 3.6 %collective-permute-start.1 = (bf16[256,256]{1,0:T(8,128)(2,1)S(1)}, bf16[256,256]{1,0:T(8,128)(2,1)S(1)}, u32[]{:S(2)}, u32[]{:S(2)}) collective-permute-start(bf16[256,256]{1,0:T(8,128)(2,1)S(1)} %collective-permute-done), channel_id=1, source_target_pairs={{0,7},{1,0},{2,1},{3,2},{4,3},{5,4},{6,5},{7,6},{8,15},{9,8},{10,9... | collective-permute-start | bytes 393224 | tf_op jit(solution)/shard_map/ppermute | solution.py:39
  20.8 9.4 %collective-permute-start.2 = (bf16[512,256]{1,0:T(8,128)(2,1)S(1)}, bf16[512,256]{1,0:T(8,128)(2,1)S(1)}, u32[]{:S(2)}, u32[]{:S(2)}) collective-permute-start(bf16[512,256]{1,0:T(8,128)(2,1)S(1)} %pad_maximum_fusion.2), channel_id=1, source_target_pairs={{0,6},{1,7},{2,0},{3,1},{4,2},{5,3},{6,4},{7,5},{8,14},{9,15},{10,... | collective-permute-start | bytes 786440 | tf_op jit(solution)/shard_map/ppermute | solution.py:39
  30.3 17.0 %collective-permute-start.3 = (bf16[1024,256]{1,0:T(8,128)(2,1)S(1)}, bf16[1024,256]{1,0:T(8,128)(2,1)S(1)}, u32[]{:S(2)}, u32[]{:S(2)}) collective-permute-start(bf16[1024,256]{1,0:T(8,128)(2,1)S(1)} %pad_maximum_fusion.1), channel_id=1, source_target_pairs={{0,4},{1,5},{2,6},{3,7},{4,0},{5,1},{6,2},{7,3},{8,12},{9,13},{10,... | collective-permute-start | bytes 1572872 | tf_op jit(solution)/shard_map/ppermute | solution.py:39
  78.0 10.6 %copy-start.4 = (u32[32]{0:T(128)S(1)}, u32[32]{0:T(128)}, u32[]{:S(2)}) copy-start(u32[32]{0:T(128)} %constant.136) | copy-start | bytes 388
  88.5 6.1 %collective-permute-start.4 = (f32[8,256]{1,0:T(8,128)S(1)}, f32[8,256]{1,0:T(8,128)S(1)}, u32[]{:S(2)}, u32[]{:S(2)}) collective-permute-start(f32[8,256]{1,0:T(8,128)S(1)} %slice.29), channel_id=1, source_target_pairs={{0,8},{8,16},{16,24},{24,0},{1,9},{9,17},{17,25},{25,1},{2,10},{10... | collective-permute-start | bytes 24584 | tf_op jit(solution)/shard_map/ppermute | solution.py:13
  109.5 9.7 %collective-permute-start.5 = (f32[1,256]{1,0:T(1,128)S(1)}, f32[1,256]{1,0:T(1,128)S(1)}, u32[]{:S(2)}, u32[]{:S(2)}) collective-permute-start(f32[1,256]{1,0:T(1,128)S(1)} %dynamic-slice_divide_fusion.1), channel_id=1, source_target_pairs={{0,24},{8,0},{16,8},{24,16},{1,25},{9,1},{17,9},{25,17},{2,26},{10... | collective-permute-start | bytes 3080 | tf_op jit(solution)/shard_map/ppermute | solution.py:13
  149.6 5.5 %collective-permute-start.6 = (f32[8,256]{1,0:T(8,128)S(1)}, f32[8,256]{1,0:T(8,128)S(1)}, u32[]{:S(2)}, u32[]{:S(2)}) collective-permute-start(f32[8,256]{1,0:T(8,128)S(1)} %slice.31), channel_id=1, source_target_pairs={{0,8},{8,16},{16,24},{24,0},{1,9},{9,17},{17,25},{25,1},{2,10},{10... | collective-permute-start | bytes 24584 | tf_op jit(solution)/shard_map/ppermute | solution.py:13
Sparse Core Ops, SparseCore 0:
  18.4 29.6 all-gather.3
